TPU v7x, 32 devices: a whole 2x2x4 slice. The times are simulated.
32 devices in a mesh: row: 4 (over y, core), col: 8 (over z, x).
Axes of the slice: x: 2, y: 2, z: 4, core: 2. Of those that a mesh axis runs over, the one named last changes fastest.
Arguments:
- shell_velocity: bfloat16 [256, 128, 128], P(('row', 'col')), may hold values from -6 to 6
- coupling: bfloat16 [256, 2, 2, 256, 128], P(('row', 'col')), may hold values from -0.375 to 0.375
- coupling_dest: int32 [256, 2], P(('row', 'col')), may hold values from 0 to 7, all different within a row; in each aligned block of 8 rows (0 to 7, 8 to 15, ...) at most 2 rows name the same one
- coupling_cluster: int32 [256, 2], P(('row', 'col')), may hold values from 0 to 63
- near_blocks: bfloat16 [4, 8, 32, 2, 256, 256], P('row', 'col'), may hold values from -0.0625 to 0.0625
- far_v: bfloat16 [4, 8, 64, 2, 32, 256], P('row', 'col'), may hold values from -0.25 to 0.25
- far_u: bfloat16 [4, 8, 64, 2, 32, 256], P('row', 'col'), may hold values from -0.125 to 0.125
- block_pairs: int32 [4, 8, 96], P('row', 'col'), may hold values from 0 to 1023, as said below
Outputs:
- response: bfloat16 [16384, 128], P(('row', 'col'))
Inputs may be any that keep to these rules, and one draw needn't show every extreme that they name: `coupling_dest`: the rows of one device name any column group at most 2 times, and some device names one exactly 2 times; the 2 entries of a row differ. `block_pairs`: each entry codes a row cluster r and column cluster c of its group as r * 64 + c; the entries of one group are distinct.
All inputs are finite; a program needn't handle non-finite values.
Results may differ from a plain program's by a relative error of at most 0.008.
Values may be sent and summed in bfloat16 or wider, within the bound.
A program may use at most 128 MiB of HBM per device.

v0:
```python
import jax
import jax.numpy as jnp
from jax import lax
from jax.sharding import PartitionSpec as P

RC_DEV = 16
CC_DEV = 64
NEAR_DEV = 32


def rotate_blocks(values, load_count):
    return jnp.concatenate([-values[..., load_count:], values[..., :load_count]], axis=-1)


def per_device(
    shell_velocity,
    coupling,
    coupling_dest,
    coupling_cluster,
    near_blocks,
    far_v,
    far_u,
    block_pairs,
):
    width = shell_velocity.shape[-1]
    load_count = width // 2
    shell_count = shell_velocity.shape[0]
    top_count = coupling.shape[1]
    panels = coupling.shape[3]
    contributions = jnp.einsum(
        "stpq,sqk->stpk", coupling[:, :, 0], shell_velocity, preferred_element_type=jnp.float32
    )
    contributions = contributions + jnp.einsum(
        "stpq,sqk->stpk",
        coupling[:, :, 1],
        rotate_blocks(shell_velocity, load_count),
        preferred_element_type=jnp.float32,
    )
    entries = shell_count * top_count
    flat_rows = contributions.astype(jnp.bfloat16).reshape(entries, panels * width)
    col_count = lax.axis_size("col")
    capacity = max(2, (entries + col_count - 1) // col_count)
    target = coupling_dest.reshape(entries)
    target_cluster = coupling_cluster.reshape(entries)
    onehot = (target[:, None] == jnp.arange(col_count, dtype=jnp.int32)[None, :]).astype(jnp.int32)
    before = jnp.cumsum(onehot, axis=0) - onehot
    slot_rank = jnp.sum(before * onehot, axis=1)
    slot_index = target * capacity + slot_rank
    slot_pick = jnp.arange(col_count * capacity, dtype=jnp.int32)[:, None] == slot_index[None, :]
    outgoing = jnp.dot(
        slot_pick.astype(jnp.bfloat16), flat_rows, preferred_element_type=jnp.float32
    )
    outgoing = outgoing.astype(jnp.bfloat16).reshape(col_count, capacity, panels, width)
    slot_ids = jnp.sum(slot_pick.astype(jnp.int32) * (target_cluster + 1)[None, :], axis=1) - 1
    slot_ids = slot_ids.reshape(col_count, capacity)
    incoming, got_ids = (
        lax.all_to_all(outgoing, "col", split_axis=0, concat_axis=0, tiled=True),
        lax.all_to_all(slot_ids, "col", split_axis=0, concat_axis=0, tiled=True),
    )
    cluster_pick = (
        jnp.arange(CC_DEV, dtype=jnp.int32)[:, None] == got_ids.reshape(-1)[None, :]
    ).astype(jnp.bfloat16)
    cluster_sums = jnp.dot(
        cluster_pick,
        incoming.reshape(col_count * capacity, panels * width),
        preferred_element_type=jnp.float32,
    ).reshape(CC_DEV, panels, width)
    source_share = lax.psum_scatter(cluster_sums, "row", scatter_dimension=1, tiled=True).astype(
        jnp.bfloat16
    )
    sources = lax.all_gather(source_share, "row", axis=1, tiled=True)
    pair_codes = block_pairs.reshape(-1)
    owners = pair_codes // CC_DEV
    columns = pair_codes % CC_DEV
    nearby_local = near_blocks[0, 0]
    nearby_input = sources[columns[:NEAR_DEV]]
    nearby_contribution = jnp.einsum(
        "dym,dmg->dyg", nearby_local[:, 0], nearby_input, preferred_element_type=jnp.float32
    )
    nearby_contribution = nearby_contribution + jnp.einsum(
        "dym,dmg->dyg",
        nearby_local[:, 1],
        rotate_blocks(nearby_input, load_count),
        preferred_element_type=jnp.float32,
    )
    distant_input = sources[columns[NEAR_DEV:]]
    distant_right_factor = far_v[0, 0]
    expansion_coefficients = jnp.einsum(
        "dyz,dzi->dyi",
        distant_right_factor[:, 0],
        distant_input,
        preferred_element_type=jnp.float32,
    )
    expansion_coefficients = expansion_coefficients + jnp.einsum(
        "dyz,dzi->dyi",
        distant_right_factor[:, 1],
        rotate_blocks(distant_input, load_count),
        preferred_element_type=jnp.float32,
    )
    expansion_coefficients = expansion_coefficients.astype(jnp.bfloat16)
    far_left = far_u[0, 0]
    far_term = jnp.einsum(
        "brp,brk->bpk", far_left[:, 0], expansion_coefficients, preferred_element_type=jnp.float32
    )
    far_term = far_term + jnp.einsum(
        "brp,brk->bpk",
        far_left[:, 1],
        rotate_blocks(expansion_coefficients, load_count),
        preferred_element_type=jnp.float32,
    )
    all_terms = jnp.concatenate([nearby_contribution, far_term], axis=0)
    high_part = all_terms.astype(jnp.bfloat16)
    low_part = (all_terms - high_part.astype(jnp.float32)).astype(jnp.bfloat16)
    owner_pick = (jnp.arange(RC_DEV, dtype=jnp.int32)[:, None] == owners[None, :]).astype(
        jnp.bfloat16
    )
    row_sums = jnp.einsum("ib,bpk->ipk", owner_pick, high_part, preferred_element_type=jnp.float32)
    row_sums = row_sums + jnp.einsum(
        "ib,bpk->ipk", owner_pick, low_part, preferred_element_type=jnp.float32
    )
    row_sums = row_sums.reshape(RC_DEV * panels, width)
    return lax.psum_scatter(row_sums, "col", scatter_dimension=0, tiled=True).astype(jnp.bfloat16)


def solution(mesh):
    return jax.shard_map(
        per_device,
        mesh=mesh,
        in_specs=(
            P(("row", "col"), None, None),
            P(("row", "col"), None, None, None, None),
            P(("row", "col"), None),
            P(("row", "col"), None),
            P("row", "col", None, None, None, None),
            P("row", "col", None, None, None, None),
            P("row", "col", None, None, None, None),
            P("row", "col", None),
        ),
        out_specs=P(("row", "col"), None),
        check_vma=False,
    )
```

profile of v0, /device:TPU:0, one launch (start us, length us, event | category | flops | bytes accessed | tf_op | source)
XLA Modules:
  0.0 330.5 jit_solution(13551763512401435682)
XLA Ops:
  9.5 7.3 %all-to-all-start = ((s32[8,1,2]{2,1,0:T(1,128)}), s32[8,1,2]{2,1,0:T(1,128)S(1)}, u32[]{:S(2)}, u32[]{:S(2)}) async-start(s32[8,1,2]{2,1,0:T(1,128)} %bitcast.2), calls=%async_computation | async-start | bytes 8192 | tf_op jit(solution)/shard_map/all_to_all | solution.py:58
  23.2 5.1 %all-to-all-start.1 = ((bf16[8,2,256,128]{3,2,1,0:T(8,128)(2,1)}), bf16[8,2,256,128]{3,2,1,0:T(8,128)(2,1)S(1)}, u32[]{:S(2)}, u32[]{:S(2)}) async-start(bf16[8,2,256,128]{3,2,1,0:T(8,128)(2,1)} %bitcast.38), calls=%async_computation.1 | async-start | bytes 2097152 | tf_op jit(solution)/shard_map/all_to_all | solution.py:57
  29.6 24.1 %all-to-all-done.1 = bf16[8,2,256,128]{3,2,1,0:T(8,128)(2,1)S(1)} async-done(((bf16[8,2,256,128]{3,2,1,0:T(8,128)(2,1)}), bf16[8,2,256,128]{3,2,1,0:T(8,128)(2,1)S(1)}, u32[]{:S(2)}, u32[]{:S(2)}) %all-to-all-start.1) | async-done | bytes 1048608 | tf_op jit(solution)/shard_map/all_to_all | solution.py:57
  53.7 4.6 %fusion.15 = f32[64,256,128]{2,0,1:T(8,128)} fusion(s32[16]{0:T(128)S(1)} %eq.66, bf16[2,8,256,128]{3,2,1,0:T(8,128)(2,1)S(1)} %bitcast.119), kind=kOutput, calls=%fused_computation.32 | convolution fusion | flops 67109888 | bytes 9437248 | tf_op jit(solution)/shard_map/dot_general | solution.py:63
  58.4 70.3 %reduce-scatter.3.cloned.1.call-done = f32[64,64,128]{2,0,1:T(8,128)} async-done(((f32[64,256,128]{2,0,1:T(8,128)}), f32[64,64,128]{2,0,1:T(8,128)}) %reduce-scatter.3.cloned.1.call-update) | async-done | bytes 2097168 | tf_op jit(solution)/shard_map/reduce_scatter | solution.py:68
  128.7 2.8 convert_element_type.37
  135.6 8.1 %copy.112 = bf16[1,1,32,2,256,256]{5,4,2,3,1,0:T(8,128)(2,1)} copy(bf16[1,1,32,2,256,256]{5,4,3,2,1,0:T(8,128)(2,1)} %param.12) | data formatting | bytes 16777216 | tf_op args[4]
  143.9 22.3 %all-gather.2.cloned.1.call-done = bf16[64,256,128]{2,0,1:T(8,128)(2,1)} async-done(((bf16[64,64,128]{2,0,1:T(8,128)(2,1)}), bf16[64,256,128]{2,0,1:T(8,128)(2,1)}) %all-gather.2.cloned.1.call-update) | async-done | bytes 4194320 | tf_op jit(solution)/shard_map/all_gather | solution.py:71
  166.2 6.8 %copy.73 = bf16[64,256,128]{2,1,0:T(8,128)(2,1)} copy(bf16[64,256,128]{2,0,1:T(8,128)(2,1)} %all-gather.2.cloned.1.call-done) | data formatting | bytes 8388608 | tf_op jit(solution)/shard_map/all_gather | solution.py:71
  173.0 3.1 gather_fusion
  176.1 5.2 %gather_fusion.1 = bf16[64,256,128]{2,1,0:T(8,128)(2,1)} fusion(bf16[64,256,128]{2,1,0:T(8,128)(2,1)} %copy.73, s32[1024]{0:T(1024)S(1)} %pad_clamp_fusion), kind=kCustom, calls=%fused_computation.1 | custom fusion | bytes 8388864 | tf_op jit(solution)/shard_map/gather | solution.py:86
  181.4 2.9 fusion.45
  189.3 4.0 %fusion.1 = f32[32,128,256]{2,1,0:T(8,128)S(1)} fusion(bf16[32,2,256,256]{3,2,0,1:T(8,128)(2,1)} %bitcast.110, bf16[32,256,64]{1,2,0:T(8,128)(2,1)S(1)} %copy.93, bf16[32,256,64]{1,2,0:T(8,128)(2,1)} %neg.13), kind=kOutput, calls=%fused_computation.10 | convolution fusion | flops 541065216 | bytes 10485760 | tf_op jit(solution)/shard_map/dym,dmg->dyg/dot_general | solution.py:80
  193.3 5.8 %add_bitcast_fusion.1 = f32[32,256,128]{1,2,0:T(8,128)} fusion(f32[32,128,256]{2,1,0:T(8,128)S(1)} %fusion.1, bf16[32,256,128]{2,1,0:T(8,128)(2,1)S(1)} %gather_fusion, bf16[32,2,256,256]{3,2,0,1:T(8,128)(2,1)} %bitcast.111), kind=kOutput, calls=%fused_computation.17 | convolution fusion | flops 537919488 | bytes 14680064 | tf_op jit(solution)/shard_map/dym,dmg->dyg/dot_general | solution.py:77
  199.1 2.0 slice_negate_fusion
  201.1 2.3 fusion.3
  206.4 5.0 %add_bitcast_fusion = f32[64,256,128]{1,2,0:T(8,128)} fusion(f32[64,128,256]{2,1,0:T(8,128)S(1)} %fusion.18, bf16[64,2,32,256]{3,2,0,1:T(8,128)(2,1)S(1)} %bitcast.113, bf16[64,32,64]{2,1,0:T(8,128)(2,1)S(1)} %get-tuple-element.10, bf16[64,32,64]{2,1,0:T(8,128)(2,1)S(1)} %get-tuple-element.9), kind=kOutput, calls=%fused_computation.7 | convolution fusion | flops 137363456 | bytes 18874368 | tf_op jit(solution)/shard_map/brp,brk->bpk/dot_general | solution.py:105
  211.4 9.0 %subtract_convert_fusion = bf16[96,256,128]{1,2,0:T(8,128)(2,1)} fusion(f32[64,256,128]{1,2,0:T(8,128)} %add_bitcast_fusion, f32[32,256,128]{1,2,0:T(8,128)} %add_bitcast_fusion.1), kind=kLoop, calls=%fused_computation.4 | loop fusion | flops 15728640 | bytes 18874368 | tf_op jit(solution)/shard_map/convert_element_type | solution.py:113
  220.4 7.9 %fusion = bf16[96,256,128]{1,2,0:T(8,128)(2,1)} fusion(f32[64,256,128]{1,2,0:T(8,128)} %add_bitcast_fusion, f32[32,256,128]{1,2,0:T(8,128)} %add_bitcast_fusion.1), kind=kLoop, calls=%fused_computation.5 | loop fusion | flops 3145728 | bytes 18874368 | tf_op jit(solution)/shard_map/convert_element_type | solution.py:112
  228.3 9.0 %copy.81 = bf16[96,256,128]{2,0,1:T(8,128)(2,1)} copy(bf16[96,256,128]{1,2,0:T(8,128)(2,1)} %fusion) | data formatting | bytes 12582912 | tf_op jit(solution)/shard_map/convert_element_type | solution.py:112
  237.3 9.1 %copy.82 = bf16[96,256,128]{2,0,1:T(8,128)(2,1)} copy(bf16[96,256,128]{1,2,0:T(8,128)(2,1)} %subtract_convert_fusion) | data formatting | bytes 12582912 | tf_op jit(solution)/shard_map/convert_element_type | solution.py:113
  246.4 3.9 %fusion.33 = f32[16,256,128]{2,0,1:T(8,128)S(1)} fusion(bf16[96,256,128]{2,0,1:T(8,128)(2,1)} %copy.81, s32[96]{0:T(128)S(1)} %get-tuple-element.13), kind=kOutput, calls=%fused_computation.61 | convolution fusion | flops 100664832 | bytes 8388992 | tf_op jit(solution)/shard_map/ib,bpk->ipk/dot_general | solution.py:117
  251.9 2.0 copy.83
  253.9 68.5 %reduce-scatter.5.cloned.1.call-done = f32[512,128]{1,0:T(8,128)} async-done(((f32[4096,128]{1,0:T(8,128)}), f32[512,128]{1,0:T(8,128)}) %reduce-scatter.5.cloned.1.call-update) | async-done | bytes 262160 | tf_op jit(solution)/shard_map/reduce_scatter | solution.py:122
  (61 shorter events, 26.0 us)
Async XLA Ops:
  6.5 13.4 %copy-start.4 = (bf16[8,2,2,256,128]{4,3,2,1,0:T(8,128)(2,1)S(1)}, bf16[8,2,2,256,128]{4,3,2,1,0:T(8,128)(2,1)}, u32[]{:S(2)}) copy-start(bf16[8,2,2,256,128]{4,3,2,1,0:T(8,128)(2,1)} %param.9) | copy-start | bytes 6291460
  9.5 13.7 %all-to-all-start = ((s32[8,1,2]{2,1,0:T(1,128)}), s32[8,1,2]{2,1,0:T(1,128)S(1)}, u32[]{:S(2)}, u32[]{:S(2)}) async-start(s32[8,1,2]{2,1,0:T(1,128)} %bitcast.2), calls=%async_computation | async-start | bytes 8192 | tf_op jit(solution)/shard_map/all_to_all | solution.py:58
  23.2 30.5 %all-to-all-start.1 = ((bf16[8,2,256,128]{3,2,1,0:T(8,128)(2,1)}), bf16[8,2,256,128]{3,2,1,0:T(8,128)(2,1)S(1)}, u32[]{:S(2)}, u32[]{:S(2)}) async-start(bf16[8,2,256,128]{3,2,1,0:T(8,128)(2,1)} %bitcast.38), calls=%async_computation.1 | async-start | bytes 2097152 | tf_op jit(solution)/shard_map/all_to_all | solution.py:57
  28.3 100.4 %reduce-scatter.3.cloned.1.call-start = ((), (), s32[]{:S(2)}) async-start(), calls=%async_computation.4 | async-start | bytes 10485760 | tf_op jit(solution)/shard_map/reduce_scatter | solution.py:68
  58.3 73.5 %copy-start.5 = (bf16[1,1,64,2,32,256]{5,4,3,2,1,0:T(8,128)(2,1)S(1)}, bf16[1,1,64,2,32,256]{5,4,3,2,1,0:T(8,128)(2,1)}, u32[]{:S(2)}) copy-start(bf16[1,1,64,2,32,256]{5,4,3,2,1,0:T(8,128)(2,1)} %param.13) | copy-start | bytes 6291460
  58.4 107.8 %all-gather.2.cloned.1.call-start = ((), (), s32[]{:S(2)}) async-start(), calls=%async_computation.5 | async-start | bytes 5242880 | tf_op jit(solution)/shard_map/all_gather | solution.py:71
  131.6 190.8 %reduce-scatter.5.cloned.1.call-start = ((), (), s32[]{:S(2)}) async-start(), calls=%async_computation.6 | async-start | bytes 2359296 | tf_op jit(solution)/shard_map/reduce_scatter | solution.py:122
  131.8 2.4 copy-start.6
  135.6 8.1 %copy-start.7 = (s32[1,1,96]{2,1,0:T(1,128)S(1)}, s32[1,1,96]{2,1,0:T(1,128)}, u32[]{:S(2)}) copy-start(s32[1,1,96]{2,1,0:T(1,128)} %param.15) | copy-start | bytes 1156
  193.3 5.9 %copy-start = (bf16[64,256,128]{2,1,0:T(8,128)(2,1)S(1)}, bf16[64,256,128]{2,1,0:T(8,128)(2,1)}, u32[]{:S(2)}) copy-start(bf16[64,256,128]{2,1,0:T(8,128)(2,1)} %gather_fusion.1) | copy-start | bytes 12582916
  199.1 2.0 copy-start.3
  203.5 1.6 copy-start.2
  246.4 4.6 %copy-start.1 = (bf16[96,256,128]{2,0,1:T(8,128)(2,1)S(1)}, bf16[96,256,128]{2,0,1:T(8,128)(2,1)}, u32[]{:S(2)}) copy-start(bf16[96,256,128]{2,0,1:T(8,128)(2,1)} %copy.82) | copy-start | bytes 18874372
Sparse Core Ops, SparseCore 0:
  58.5 70.2 reduce-scatter.2
  131.7 34.4 all-gather.1
  254.1 68.2 reduce-scatter.4
where the time goes:
time: 332 us; the launch traced here: 331 us
  waiting for transfers between devices  186 us (56%)
  local copies, waits for them, and re-layouts  60.1 us (18%)
  matrix products  31.5 us (9%)
  other arithmetic  26.8 us (8%)
  between operations  13.3 us (4%)
  starting transfers between devices  12.7 us (4%)
    reduce_scatter x1, waiting for transfers between devices, per_device(): lax.psum_scatter(cluster_sums, 'row', scatter_dimension=1, tiled=True)  70.3 us
    reduce_scatter x1, waiting for transfers between devices, per_device(): lax.psum_scatter(row_sums, 'col', scatter_dimension=0, tiled=True)  68.5 us
    all_to_all x1, waiting for transfers between devices, per_device(): lax.all_to_all(outgoing, 'col', split_axis=0, concat_axis=0, tiled=True)  24.1 us
    all_gather x1, waiting for transfers between devices, per_device(): sources = lax.all_gather(source_share, 'row', axis=1, tiled=True)  22.3 us
    unnamed x25, local copies, waits for them, and re-layouts  19.2 us
    convert_element_type x1, local copies, waits for them, and re-layouts, per_device(): low_part = (all_terms - high_part.astype(jnp.float32)).astype(jnp.bfloat16)  9.1 us
    convert_element_type x1, local copies, waits for them, and re-layouts, per_device(): high_part = all_terms.astype(jnp.bfloat16)  9.03 us
    convert_element_type x1, other arithmetic, per_device(): low_part = (all_terms - high_part.astype(jnp.float32)).astype(jnp.bfloat16)  9.01 us
  transfers between devices with their start and end apart: 5, of which 5 were waited for; matrix products, arithmetic and copies ran while one was open for 5% of the time, Pallas kernels for 0%

commit v1 on v0

v1 whole, which is shorter than its diff:
```python
import functools

import jax
import jax.numpy as jnp
from jax import lax
from jax.experimental import pallas as pl
from jax.experimental.pallas import tpu as pltpu
from jax.sharding import PartitionSpec as P

RC_DEV = 16
CC_DEV = 64
NEAR_DEV = 32
CORES = 2
TAIL = 16
MESH = pl.DeviceIdType.MESH


def rotate(values):
    half = values.shape[-1] // 2
    lane = lax.broadcasted_iota(jnp.int32, values.shape, values.ndim - 1)
    turned = pltpu.roll(values, half, values.ndim - 1)
    return jnp.where(lane < half, -turned, turned)


def flip(index, mask, size):
    result, bit = 0, 1
    while bit < size:
        result = result + bit * ((index // bit + mask // bit) % 2)
        bit *= 2
    return result


def exchange_kernel(
    rows, cols, capacity, dest_ref, cluster_ref, coupling_ref, velocity_ref, got_ref,
    outgoing, send_col, send_y, send_core, recv,
):
    g, h = lax.axis_index("row"), lax.axis_index("col")
    entries, twice, _ = coupling_ref.shape
    panels = twice // 2
    top = entries // velocity_ref.shape[0]
    peers = rows // CORES
    y, core = g // CORES, g % CORES
    mate = y * CORES + (CORES - 1 - core)

    barrier = pltpu.get_barrier_semaphore()
    for step in range(1, cols):
        pl.semaphore_signal(barrier, inc=1, device_id=(g, (h + step) % cols), device_id_type=MESH)
    for step in range(1, peers):
        pl.semaphore_signal(
            barrier, inc=1, device_id=((y + step) % peers * CORES + core, h), device_id_type=MESH
        )
    pl.semaphore_signal(barrier, inc=1, device_id=(mate, h), device_id_type=MESH)

    def fill(dst, target):
        picked = [jnp.int32(-1)] * capacity
        count = jnp.int32(0)
        for e in range(entries):
            hit = dest_ref[e] == target
            for k in range(capacity):
                picked[k] = jnp.where(hit & (count == k), e, picked[k])
            count = count + jnp.where(hit, 1, 0)
        for k in range(capacity):
            valid = picked[k] >= 0
            e = jnp.maximum(picked[k], 0)
            product = jnp.dot(
                coupling_ref[e], velocity_ref[e // top], preferred_element_type=jnp.float32
            )
            value = product[:panels] + rotate(product[panels:])
            scale = jnp.where(valid, 1.0, 0.0)
            dst[k, pl.ds(0, panels), :] = (value * scale).astype(jnp.bfloat16)
            number = jnp.where(valid, cluster_ref[e], 0).astype(jnp.float32)
            dst[k, pl.ds(panels, TAIL), :] = jnp.full(
                (TAIL, value.shape[-1]), number, jnp.float32
            ).astype(jnp.bfloat16)

    def col_copy(j):
        target = flip(h, j, cols)
        return pltpu.make_async_remote_copy(
            src_ref=outgoing.at[j],
            dst_ref=got_ref.at[g, h],
            send_sem=send_col.at[j],
            recv_sem=recv.at[g, h],
            device_id=(g, target),
            device_id_type=MESH,
        )

    def y_copy(step, j):
        source = flip(h, j, cols)
        return pltpu.make_async_remote_copy(
            src_ref=got_ref.at[g, source],
            dst_ref=got_ref.at[g, source],
            send_sem=send_y.at[step, j],
            recv_sem=recv.at[g, source],
            device_id=((y + step) % peers * CORES + core, h),
            device_id_type=MESH,
        )

    def core_copy(step, j):
        source = flip(h, j, cols)
        origin = (y + step) % peers * CORES + core
        return pltpu.make_async_remote_copy(
            src_ref=got_ref.at[origin, source],
            dst_ref=got_ref.at[origin, source],
            send_sem=send_core.at[step, j],
            recv_sem=recv.at[origin, source],
            device_id=(mate, h),
            device_id_type=MESH,
        )

    def arrived(origin, j):
        source = flip(h, j, cols)
        pltpu.make_async_copy(
            got_ref.at[origin, source], got_ref.at[origin, source], recv.at[origin, source]
        ).wait()

    fill(got_ref.at[g, h], h)
    pl.semaphore_wait(barrier, cols - 1 + peers - 1 + 1)
    for step in range(1, peers):
        y_copy(step, 0).start()
    core_copy(0, 0).start()

    @pl.loop(1, cols)
    def _(j):
        fill(outgoing.at[j], flip(h, j, cols))
        col_copy(j).start()

    lag = cols // 2

    def relay(j):
        for step in range(1, peers):
            arrived((y + step) % peers * CORES + core, j)
            core_copy(step, j).start()

    @pl.loop(1, lag)
    def _(j):
        arrived(g, j)
        for step in range(1, peers):
            y_copy(step, j).start()
        core_copy(0, j).start()

    @pl.loop(lag, cols)
    def _(j):
        arrived(g, j)
        for step in range(1, peers):
            y_copy(step, j).start()
        core_copy(0, j).start()
        relay(j - lag)

    @pl.loop(cols - lag, cols)
    def _(j):
        relay(j)

    @pl.loop(0, cols)
    def _(j):
        for step in range(peers):
            arrived((y + step) % peers * CORES + (CORES - 1 - core), j)

    @pl.loop(1, cols)
    def _(j):
        col_copy(j).wait_send()

    @pl.loop(0, cols)
    def _(j):
        for step in range(1, peers):
            y_copy(step, j).wait_send()
        for step in range(peers):
            core_copy(step, j).wait_send()


def field_kernel(
    steps, ids_ref, pairs_ref, got_ref, near_ref, v_ref, u_ref, out_ref,
    head, link, sources, total,
):
    step = pl.program_id(0)
    slots, _, width = got_ref.shape
    near_count, twice, panels = near_ref.shape
    far_count, rank2, _ = v_ref.shape
    rank = rank2 // 2

    @pl.when(step == 0)
    def _():
        @pl.loop(0, CC_DEV)
        def _(c):
            head[c] = -1

        @pl.loop(0, slots)
        def _(n):
            c = ids_ref[n]
            link[n] = head[c]
            head[c] = n

        @pl.loop(0, CC_DEV)
        def _(c):
            def more(state):
                return state[0] >= 0

            def add(state):
                n, value = state
                return link[n], value + got_ref[n, pl.ds(0, panels), :].astype(jnp.float32)

            _, value = lax.while_loop(
                more, add, (head[c], jnp.zeros((panels, width), jnp.float32))
            )
            sources[c] = value.astype(jnp.bfloat16)

        total[...] = jnp.zeros_like(total)

    for b in range(near_count):
        code = pairs_ref[step * near_count + b]
        total[code // CC_DEV] += jnp.dot(
            near_ref[b], sources[code % CC_DEV], preferred_element_type=jnp.float32
        )

    for b in range(far_count):
        code = pairs_ref[steps * near_count + step * far_count + b]
        part = jnp.dot(v_ref[b], sources[code % CC_DEV], preferred_element_type=jnp.float32)
        coeffs = part[:rank] + rotate(part[rank:])
        both = jnp.concatenate([coeffs, rotate(coeffs)], axis=0).astype(jnp.bfloat16)
        total[code // CC_DEV, pl.ds(0, panels), :] += lax.dot_general(
            u_ref[b], both, (((0,), (0,)), ((), ())), preferred_element_type=jnp.float32
        )

    @pl.when(step == steps - 1)
    def _():
        @pl.loop(0, RC_DEV)
        def _(r):
            value = total[r, pl.ds(0, panels), :] + rotate(total[r, pl.ds(panels, panels), :])
            out_ref[r] = value.astype(jnp.bfloat16)


def reduce_kernel(
    zs, xs, part_ref, out_ref, first, middle, second, send1, recv1, send2, recv2
):
    g, h = lax.axis_index("row"), lax.axis_index("col")
    z, x = h // xs, h % xs

    barrier = pltpu.get_barrier_semaphore()
    for d in range(1, xs):
        pl.semaphore_signal(
            barrier, inc=1, device_id=(g, z * xs + (x + d) % xs), device_id_type=MESH
        )
    for k in range(1, zs):
        pl.semaphore_signal(
            barrier, inc=1, device_id=(g, (z + k) % zs * xs + x), device_id_type=MESH
        )
    pl.semaphore_wait(barrier, xs - 1 + zs - 1)

    def x_copy(k, d):
        goal, other = flip(z, k, zs), (x + d) % xs
        return pltpu.make_async_remote_copy(
            src_ref=part_ref.at[goal * xs + other],
            dst_ref=first.at[goal, x],
            send_sem=send1.at[goal, other],
            recv_sem=recv1.at[goal, x],
            device_id=(g, z * xs + other),
            device_id_type=MESH,
        )

    def z_copy(k):
        goal = flip(z, k, zs)
        return pltpu.make_async_remote_copy(
            src_ref=middle.at[goal],
            dst_ref=second.at[z],
            send_sem=send2.at[goal],
            recv_sem=recv2.at[z],
            device_id=(g, goal * xs + x),
            device_id_type=MESH,
        )

    for k in reversed(range(zs)):
        for d in range(1, xs):
            x_copy(k, d).start()
    for k in reversed(range(zs)):
        goal = flip(z, k, zs)
        value = part_ref[goal * xs + x].astype(jnp.float32)
        for d in range(1, xs):
            other = (x + d) % xs
            pltpu.make_async_copy(
                first.at[goal, other], first.at[goal, other], recv1.at[goal, other]
            ).wait()
            value = value + first[goal, other].astype(jnp.float32)
        if k:
            middle[goal] = value.astype(jnp.bfloat16)
            z_copy(k).start()
    for k in range(1, zs):
        source = flip(z, k, zs)
        pltpu.make_async_copy(second.at[source], second.at[source], recv2.at[source]).wait()
        value = value + second[source].astype(jnp.float32)
    out_ref[...] = value.astype(jnp.bfloat16)
    for k in range(zs):
        for d in range(1, xs):
            x_copy(k, d).wait_send()
        if k:
            z_copy(k).wait_send()


def per_device(
    row_count, col_count,
    shell_velocity, coupling, coupling_dest, coupling_cluster, near_blocks, far_v, far_u,
    block_pairs,
):
    width = shell_velocity.shape[-1]
    shells, top, _, panels, depth = coupling.shape
    entries = shells * top
    capacity = max(2, (entries + col_count - 1) // col_count)
    peers = row_count // CORES
    message = (capacity, panels + TAIL, width)
    vmem = pl.BlockSpec(memory_space=pltpu.VMEM)
    smem = pl.BlockSpec(memory_space=pltpu.SMEM)
    dma = pltpu.SemaphoreType.DMA

    got = pl.pallas_call(
        functools.partial(exchange_kernel, row_count, col_count, capacity),
        out_shape=jax.ShapeDtypeStruct((row_count, col_count) + message, jnp.bfloat16),
        in_specs=[smem, smem, vmem, vmem],
        out_specs=vmem,
        scratch_shapes=[
            pltpu.VMEM((col_count,) + message, jnp.bfloat16),
            dma((col_count,)),
            dma((peers, col_count)),
            dma((peers, col_count)),
            dma((row_count, col_count)),
        ],
        compiler_params=pltpu.CompilerParams(
            collective_id=0, has_side_effects=True, vmem_limit_bytes=48 * 1024 * 1024
        ),
        name="exchange",
    )(
        coupling_dest.reshape(entries),
        coupling_cluster.reshape(entries),
        coupling.reshape(entries, 2 * panels, depth),
        shell_velocity,
    )

    slots = row_count * col_count * capacity
    got = got.reshape(slots, panels + TAIL, width)
    ids = got[:, panels, 0].astype(jnp.int32)
    near_count, far_count, rank = near_blocks.shape[2], far_v.shape[2], far_v.shape[4]
    near = near_blocks.reshape(near_count, 2 * panels, panels)
    right = far_v.reshape(far_count, 2 * rank, panels)
    left = far_u.reshape(far_count, 2 * rank, panels)
    steps = 8
    partial_rows = pl.pallas_call(
        functools.partial(field_kernel, steps),
        grid=(steps,),
        out_shape=jax.ShapeDtypeStruct((RC_DEV, panels, width), jnp.bfloat16),
        in_specs=[
            smem,
            smem,
            vmem,
            pl.BlockSpec((near_count // steps, 2 * panels, panels), lambda i: (i, 0, 0)),
            pl.BlockSpec((far_count // steps, 2 * rank, panels), lambda i: (i, 0, 0)),
            pl.BlockSpec((far_count // steps, 2 * rank, panels), lambda i: (i, 0, 0)),
        ],
        out_specs=pl.BlockSpec((RC_DEV, panels, width), lambda i: (0, 0, 0)),
        scratch_shapes=[
            pltpu.SMEM((CC_DEV,), jnp.int32),
            pltpu.SMEM((slots,), jnp.int32),
            pltpu.VMEM((CC_DEV, panels, width), jnp.bfloat16),
            pltpu.VMEM((RC_DEV, 2 * panels, width), jnp.float32),
        ],
        compiler_params=pltpu.CompilerParams(vmem_limit_bytes=56 * 1024 * 1024),
        name="fields",
    )(ids, block_pairs.reshape(-1), got, near, right, left)

    out_rows = RC_DEV * panels // col_count
    xs = 1
    while 4 * xs * xs <= col_count:
        xs *= 2
    zs = col_count // xs
    return pl.pallas_call(
        functools.partial(reduce_kernel, zs, xs),
        out_shape=jax.ShapeDtypeStruct((out_rows, width), jnp.bfloat16),
        in_specs=[vmem],
        out_specs=vmem,
        scratch_shapes=[
            pltpu.VMEM((zs, xs, out_rows, width), jnp.bfloat16),
            pltpu.VMEM((zs, out_rows, width), jnp.bfloat16),
            pltpu.VMEM((zs, out_rows, width), jnp.bfloat16),
            dma((zs, xs)),
            dma((zs, xs)),
            dma((zs,)),
            dma((zs,)),
        ],
        compiler_params=pltpu.CompilerParams(
            collective_id=1, has_side_effects=True, vmem_limit_bytes=32 * 1024 * 1024
        ),
        name="reduce",
    )(partial_rows.reshape(col_count, out_rows, width))


def solution(mesh):
    return jax.shard_map(
        functools.partial(per_device, mesh.shape["row"], mesh.shape["col"]),
        mesh=mesh,
        in_specs=(
            P(("row", "col"), None, None),
            P(("row", "col"), None, None, None, None),
            P(("row", "col"), None),
            P(("row", "col"), None),
            P("row", "col", None, None, None, None),
            P("row", "col", None, None, None, None),
            P("row", "col", None, None, None, None),
            P("row", "col", None),
        ),
        out_specs=P(("row", "col"), None),
        check_vma=False,
    )
```

time: 332 us -> 94.3 us (0.28)
  waiting for transfers between devices: 186 us -> 0 us
  Pallas kernels: 0 us -> 85.3 us
  local copies, waits for them, and re-layouts: 60.1 us -> 6.1 us
  matrix products: 31.5 us -> 0 us
  other arithmetic: 26.8 us -> 2.65 us
  between operations: 13.3 us -> 0.02 us
  starting transfers between devices: 12.7 us -> 0 us
    reduce_scatter x2 -> x0, waiting for transfers between devices: 139 us -> none  [the longest x1 70.3 us: per_device(): lax.psum_scatter(cluster_sums, 'row', scatter_dimension=1, tiled=True)]
    pallas_call x0 -> x3, Pallas kernels: none -> 85.3 us  [the longest x1 40.4 us: per_device(): pl.pallas_call(functools.partial(exchange_kernel, row_count, col_count, c...]
    dot_general x12 -> x0, matrix products: 31.5 us -> none  [the longest x1 5.84 us: per_device(): jnp.einsum('dym,dmg->dyg', nearby_local[:, 0], nearby_input, preferred_el...]
    all_to_all x2 -> x0, waiting for transfers between devices: 25 us -> none  [the longest x1 24.1 us: per_device(): lax.all_to_all(outgoing, 'col', split_axis=0, concat_axis=0, tiled=True)]
    all_gather x1 -> x0, waiting for transfers between devices: 22.3 us -> none  [per_device(): sources = lax.all_gather(source_share, 'row', axis=1, tiled=True)]
    convert_element_type x5 -> x1, other arithmetic: 21.4 us -> 2.65 us  [per_device(): ids = got[:, panels, 0].astype(jnp.int32)]
    convert_element_type x2 -> x0, local copies, waits for them, and re-layouts: 18.1 us -> none  [the longest x1 9.1 us: per_device(): low_part = (all_terms - high_part.astype(jnp.float32)).astype(jnp.bfloat16)]
    unnamed x25 -> x9, local copies, waits for them, and re-layouts: 19.2 us -> 5.93 us
  transfers between devices with their start and end apart: 5 -> 0, of which waited for: 5 -> 0; matrix products, arithmetic and copies ran while one was open for 5% -> 0% of each run, Pallas kernels for 0% -> 0%
where the time goes in v1:
time: 94.3 us; the launch traced here: 94 us
  Pallas kernels  85.3 us (90%)
  local copies, waits for them, and re-layouts  6.1 us (6%)
  other arithmetic  2.65 us (3%)
    pallas_call x1, Pallas kernels, per_device(): pl.pallas_call(functools.partial(exchange_kernel, row_count, col_count, c...  40.4 us
    pallas_call x1, Pallas kernels, per_device(): pl.pallas_call(functools.partial(field_kernel, steps), grid=(steps,), out...  23.7 us
    pallas_call x1, Pallas kernels, per_device(): pl.pallas_call(functools.partial(reduce_kernel, zs, xs), out_shape=jax.Sh...  21.2 us
    unnamed x9, local copies, waits for them, and re-layouts  5.93 us
    convert_element_type x1, other arithmetic, per_device(): ids = got[:, panels, 0].astype(jnp.int32)  2.65 us

profile of v1, /device:TPU:0, one launch (start us, length us, event | category | flops | bytes accessed | tf_op | source)
XLA Modules:
  0.0 94.0 jit_solution(13726132202287188851)
XLA Ops:
  0.0 0.8 copy.11
  0.8 0.1 reshape.29.dest_ref
  0.8 0.8 copy.12
  1.6 0.1 reshape.30.cluster_ref
  1.7 0.0 copy-start.1
  1.7 1.6 %copy-done.1 = bf16[8,2,2,256,128]{4,3,2,1,0:T(8,128)(2,1)S(1)} copy-done((bf16[8,2,2,256,128]{4,3,2,1,0:T(8,128)(2,1)S(1)}, bf16[8,2,2,256,128]{4,3,2,1,0:T(8,128)(2,1)}, u32[]{:S(2)}) %copy-start.1) | copy-done | bytes 2097176
  3.3 0.0 copy-start.2
  3.3 0.9 %copy-done.2 = bf16[8,128,128]{2,1,0:T(8,128)(2,1)S(1)} copy-done((bf16[8,128,128]{2,1,0:T(8,128)(2,1)S(1)}, bf16[8,128,128]{2,1,0:T(8,128)(2,1)}, u32[]{:S(2)}) %copy-start.2) | copy-done | bytes 262168
  4.2 40.4 %exchange.1 = bf16[4,8,2,272,128]{4,3,2,1,0:T(8,128)(2,1)} custom-call(s32[16]{0:T(128)S(1)} %reshape.29.dest_ref, s32[16]{0:T(128)S(1)} %reshape.30.cluster_ref, bf16[16,512,128]{2,1,0:T(8,128)(2,1)S(1)} %bitcast.8, bf16[8,128,128]{2,1,0:T(8,128)(2,1)S(1)} %copy-done.2), custom_call_target="tpu_custom_call" | custom-call | tf_op jit(solution)/shard_map/exchange/pallas_call | solution.py:312
  44.6 2.6 %fusion.ids_ref = s32[64]{0:T(128)} fusion(bf16[64,272,128]{2,1,0:T(8,128)(2,1)} %bitcast.9), kind=kLoop, calls=%fused_computation.1 | loop fusion | flops 64 | bytes 384 | tf_op jit(solution)/shard_map/convert_element_type | solution.py:337
  47.3 23.7 %fields.1 = bf16[16,256,128]{2,1,0:T(8,128)(2,1)} custom-call(s32[64]{0:T(128)} %fusion.ids_ref, s32[96]{0:T(128)} %bitcast.14, bf16[64,272,128]{2,1,0:T(8,128)(2,1)} %bitcast.10, bf16[32,512,256]{2,1,0:T(8,128)(2,1)} %bitcast.11, bf16[64,64,256]{2,1,0:T(8,128)(2,1)} %bitcast.12, bf16[64,64,256]{2,1,0:T(8,128)(2,1)} %bitcast.13), custom_call_target="tpu_custom_call" | custom-call | tf_op jit(solution)/shard_map/fields/pallas_call | solution.py:343
  71.0 0.0 copy-start
  71.0 1.2 %copy-done = bf16[16,256,128]{2,1,0:T(8,128)(2,1)S(1)} copy-done((bf16[16,256,128]{2,1,0:T(8,128)(2,1)S(1)}, bf16[16,256,128]{2,1,0:T(8,128)(2,1)}, u32[]{:S(2)}) %copy-start) | copy-done | bytes 1048600
  72.2 21.2 %reduce.3 = bf16[512,128]{1,0:T(8,128)(2,1)S(1)} custom-call(bf16[8,512,128]{2,1,0:T(8,128)(2,1)S(1)} %bitcast.7), custom_call_target="tpu_custom_call" | custom-call | tf_op jit(solution)/shard_map/reduce/pallas_call | solution.py:371
  93.4 0.7 copy.14
Async XLA Ops:
  1.7 1.6 %copy-start.1 = (bf16[8,2,2,256,128]{4,3,2,1,0:T(8,128)(2,1)S(1)}, bf16[8,2,2,256,128]{4,3,2,1,0:T(8,128)(2,1)}, u32[]{:S(2)}) copy-start(bf16[8,2,2,256,128]{4,3,2,1,0:T(8,128)(2,1)} %param.9) | copy-start | bytes 6291460
  3.3 0.9 %copy-start.2 = (bf16[8,128,128]{2,1,0:T(8,128)(2,1)S(1)}, bf16[8,128,128]{2,1,0:T(8,128)(2,1)}, u32[]{:S(2)}) copy-start(bf16[8,128,128]{2,1,0:T(8,128)(2,1)} %velocity_ref.1) | copy-start | bytes 786436
  71.0 1.2 %copy-start = (bf16[16,256,128]{2,1,0:T(8,128)(2,1)S(1)}, bf16[16,256,128]{2,1,0:T(8,128)(2,1)}, u32[]{:S(2)}) copy-start(bf16[16,256,128]{2,1,0:T(8,128)(2,1)} %fields.1) | copy-start | bytes 3145732

commit v2 on v1

--- a/solution.py
+++ b/solution.py
@@ -31,16 +31,25 @@
 
 
 def exchange_kernel(
-    rows, cols, capacity, dest_ref, cluster_ref, coupling_ref, velocity_ref, got_ref,
-    outgoing, send_col, send_y, send_core, recv,
+    rows, cols, capacity, dest_ref, cluster_ref, coupling_hbm, velocity_hbm, got_ref, ids_ref,
+    coupling_ref, velocity_ref, outgoing, tails, load_sem, tail_sem, send_col, send_y,
+    send_core, recv,
 ):
     g, h = lax.axis_index("row"), lax.axis_index("col")
     entries, twice, _ = coupling_ref.shape
     panels = twice // 2
+    width = velocity_ref.shape[-1]
     top = entries // velocity_ref.shape[0]
     peers = rows // CORES
     y, core = g // CORES, g % CORES
     mate = y * CORES + (CORES - 1 - core)
+
+    loads = (
+        pltpu.make_async_copy(coupling_hbm, coupling_ref, load_sem.at[0]),
+        pltpu.make_async_copy(velocity_hbm, velocity_ref, load_sem.at[1]),
+    )
+    for load in loads:
+        load.start()
 
     barrier = pltpu.get_barrier_semaphore()
     for step in range(1, cols):
@@ -50,15 +59,20 @@
             barrier, inc=1, device_id=((y + step) % peers * CORES + core, h), device_id_type=MESH
         )
     pl.semaphore_signal(barrier, inc=1, device_id=(mate, h), device_id_type=MESH)
-
-    def fill(dst, target):
+    for load in loads:
+        load.wait()
+
+    def fill(j):
+        target = flip(h, j, cols)
         picked = [jnp.int32(-1)] * capacity
         count = jnp.int32(0)
         for e in range(entries):
-            hit = dest_ref[e] == target
+            hit = dest_ref[e // top, e % top] == target
             for k in range(capacity):
                 picked[k] = jnp.where(hit & (count == k), e, picked[k])
             count = count + jnp.where(hit, 1, 0)
+        lane = lax.broadcasted_iota(jnp.int32, (TAIL, width), 1)
+        tail = jnp.zeros((TAIL, width), jnp.float32)
         for k in range(capacity):
             valid = picked[k] >= 0
             e = jnp.maximum(picked[k], 0)
@@ -67,11 +81,10 @@
             )
             value = product[:panels] + rotate(product[panels:])
             scale = jnp.where(valid, 1.0, 0.0)
-            dst[k, pl.ds(0, panels), :] = (value * scale).astype(jnp.bfloat16)
-            number = jnp.where(valid, cluster_ref[e], 0).astype(jnp.float32)
-            dst[k, pl.ds(panels, TAIL), :] = jnp.full(
-                (TAIL, value.shape[-1]), number, jnp.float32
-            ).astype(jnp.bfloat16)
+            outgoing[j, pl.ds(k * panels, panels), :] = (value * scale).astype(jnp.bfloat16)
+            number = jnp.where(valid, cluster_ref[e // top, e % top], 0).astype(jnp.float32)
+            tail = jnp.where(lane == k, number, tail)
+        outgoing[j, pl.ds(capacity * panels, TAIL), :] = tail.astype(jnp.bfloat16)
 
     def col_copy(j):
         target = flip(h, j, cols)
@@ -84,27 +97,29 @@
             device_id_type=MESH,
         )
 
-    def y_copy(step, j):
+    def relay_copy(origin, source, block, send_sem, row):
+        return pltpu.make_async_remote_copy(
+            src_ref=block,
+            dst_ref=got_ref.at[origin, source],
+            send_sem=send_sem,
+            recv_sem=recv.at[origin, source],
+            device_id=(row, h),
+            device_id_type=MESH,
+        )
+
+    def y_copy(step, j, block=None):
         source = flip(h, j, cols)
-        return pltpu.make_async_remote_copy(
-            src_ref=got_ref.at[g, source],
-            dst_ref=got_ref.at[g, source],
-            send_sem=send_y.at[step, j],
-            recv_sem=recv.at[g, source],
-            device_id=((y + step) % peers * CORES + core, h),
-            device_id_type=MESH,
-        )
-
-    def core_copy(step, j):
+        return relay_copy(
+            g, source, got_ref.at[g, source] if block is None else block,
+            send_y.at[step, j], (y + step) % peers * CORES + core,
+        )
+
+    def core_copy(step, j, block=None):
         source = flip(h, j, cols)
         origin = (y + step) % peers * CORES + core
-        return pltpu.make_async_remote_copy(
-            src_ref=got_ref.at[origin, source],
-            dst_ref=got_ref.at[origin, source],
-            send_sem=send_core.at[step, j],
-            recv_sem=recv.at[origin, source],
-            device_id=(mate, h),
-            device_id_type=MESH,
+        return relay_copy(
+            origin, source, got_ref.at[origin, source] if block is None else block,
+            send_core.at[step, j], mate,
         )
 
     def arrived(origin, j):
@@ -113,53 +128,76 @@
             got_ref.at[origin, source], got_ref.at[origin, source], recv.at[origin, source]
         ).wait()
 
-    fill(got_ref.at[g, h], h)
+    fill(0)
+    own = pltpu.make_async_copy(outgoing.at[0], got_ref.at[g, h], send_col.at[0])
+    own.start()
     pl.semaphore_wait(barrier, cols - 1 + peers - 1 + 1)
     for step in range(1, peers):
-        y_copy(step, 0).start()
-    core_copy(0, 0).start()
+        y_copy(step, 0, outgoing.at[0]).start()
+    core_copy(0, 0, outgoing.at[0]).start()
+
+    half = cols // 2
 
     @pl.loop(1, cols)
-    def _(j):
-        fill(outgoing.at[j], flip(h, j, cols))
+    def _(i):
+        j = (i % 2) * half + i // 2
+        fill(j)
         col_copy(j).start()
 
     lag = cols // 2
 
-    def relay(j):
-        for step in range(1, peers):
-            arrived((y + step) % peers * CORES + core, j)
-            core_copy(step, j).start()
-
-    @pl.loop(1, lag)
-    def _(j):
+    def pass_on(i):
+        j = (i % 2) * half + i // 2
         arrived(g, j)
         for step in range(1, peers):
             y_copy(step, j).start()
         core_copy(0, j).start()
 
+    def relay(i):
+        j = (i % 2) * half + i // 2
+        for step in range(1, peers):
+            arrived((y + step) % peers * CORES + core, j)
+            core_copy(step, j).start()
+
+    @pl.loop(1, lag)
+    def _(i):
+        pass_on(i)
+
     @pl.loop(lag, cols)
-    def _(j):
-        arrived(g, j)
-        for step in range(1, peers):
-            y_copy(step, j).start()
-        core_copy(0, j).start()
-        relay(j - lag)
+    def _(i):
+        pass_on(i)
+        relay(i - lag)
 
     @pl.loop(cols - lag, cols)
-    def _(j):
-        relay(j)
+    def _(i):
+        relay(i)
 
     @pl.loop(0, cols)
     def _(j):
         for step in range(peers):
             arrived((y + step) % peers * CORES + (CORES - 1 - core), j)
 
+    own.wait()
+    gather = pltpu.make_async_copy(
+        got_ref.at[:, :, pl.ds(capacity * panels, TAIL), :], tails, tail_sem.at[0]
+    )
+    gather.start()
+    gather.wait()
+    for q in range(rows * cols):
+        row = tails[q // cols, q % cols].astype(jnp.float32)
+        ids_ref[pl.ds(q, 1), :] = row[:1].astype(jnp.int32)
+
     @pl.loop(1, cols)
     def _(j):
         col_copy(j).wait_send()
 
-    @pl.loop(0, cols)
+    for step in range(1, peers):
+        y_copy(step, 0, outgoing.at[0]).wait_send()
+    core_copy(0, 0, outgoing.at[0]).wait_send()
+    for step in range(1, peers):
+        core_copy(step, 0).wait_send()
+
+    @pl.loop(1, cols)
     def _(j):
         for step in range(1, peers):
             y_copy(step, j).wait_send()
@@ -168,11 +206,11 @@
 
 
 def field_kernel(
-    steps, ids_ref, pairs_ref, got_ref, near_ref, v_ref, u_ref, out_ref,
-    head, link, sources, total,
+    steps, capacity, ids_ref, pairs_ref, got_ref, near_ref, v_ref, u_ref, out_ref,
+    head, link, sources, near_total, far_total,
 ):
     step = pl.program_id(0)
-    slots, _, width = got_ref.shape
+    messages, _, width = got_ref.shape
     near_count, twice, panels = near_ref.shape
     far_count, rank2, _ = v_ref.shape
     rank = rank2 // 2
@@ -183,11 +221,12 @@
         def _(c):
             head[c] = -1
 
-        @pl.loop(0, slots)
-        def _(n):
-            c = ids_ref[n]
-            link[n] = head[c]
-            head[c] = n
+        @pl.loop(0, messages)
+        def _(q):
+            for k in range(capacity):
+                c = ids_ref[q, k]
+                link[q * capacity + k] = head[c]
+                head[c] = q * capacity + k
 
         @pl.loop(0, CC_DEV)
         def _(c):
@@ -196,43 +235,60 @@
 
             def add(state):
                 n, value = state
-                return link[n], value + got_ref[n, pl.ds(0, panels), :].astype(jnp.float32)
+                start = pl.multiple_of(n % capacity * panels, panels)
+                block = got_ref[n // capacity, pl.ds(start, panels), :]
+                return link[n], value + block.astype(jnp.float32)
 
             _, value = lax.while_loop(
                 more, add, (head[c], jnp.zeros((panels, width), jnp.float32))
             )
             sources[c] = value.astype(jnp.bfloat16)
 
-        total[...] = jnp.zeros_like(total)
+        near_total[...] = jnp.zeros_like(near_total)
+        far_total[...] = jnp.zeros_like(far_total)
+
+    codes = [pairs_ref[steps * near_count + step * far_count + b] for b in range(far_count)]
+    parts = [
+        jnp.dot(v_ref[b], sources[codes[b] % CC_DEV], preferred_element_type=jnp.float32)
+        for b in range(far_count)
+    ]
+    boths = []
+    for part in parts:
+        coeffs = part[:rank] + rotate(part[rank:])
+        boths.append(jnp.concatenate([coeffs, rotate(coeffs)], axis=0).astype(jnp.bfloat16))
 
     for b in range(near_count):
         code = pairs_ref[step * near_count + b]
-        total[code // CC_DEV] += jnp.dot(
+        near_total[code // CC_DEV] += jnp.dot(
             near_ref[b], sources[code % CC_DEV], preferred_element_type=jnp.float32
         )
 
     for b in range(far_count):
-        code = pairs_ref[steps * near_count + step * far_count + b]
-        part = jnp.dot(v_ref[b], sources[code % CC_DEV], preferred_element_type=jnp.float32)
-        coeffs = part[:rank] + rotate(part[rank:])
-        both = jnp.concatenate([coeffs, rotate(coeffs)], axis=0).astype(jnp.bfloat16)
-        total[code // CC_DEV, pl.ds(0, panels), :] += lax.dot_general(
-            u_ref[b], both, (((0,), (0,)), ((), ())), preferred_element_type=jnp.float32
+        far_total[codes[b] // CC_DEV] += lax.dot_general(
+            u_ref[b], boths[b], (((0,), (0,)), ((), ())), preferred_element_type=jnp.float32
         )
 
     @pl.when(step == steps - 1)
     def _():
         @pl.loop(0, RC_DEV)
         def _(r):
-            value = total[r, pl.ds(0, panels), :] + rotate(total[r, pl.ds(panels, panels), :])
+            value = near_total[r, pl.ds(0, panels), :] + far_total[r]
+            value = value + rotate(near_total[r, pl.ds(panels, panels), :])
             out_ref[r] = value.astype(jnp.bfloat16)
 
 
 def reduce_kernel(
-    zs, xs, part_ref, out_ref, first, middle, second, send1, recv1, send2, recv2
+    zs, xs, part_ref, out_ref, mine, first, middle, second, load_sem, send1, recv1, send2, recv2
 ):
     g, h = lax.axis_index("row"), lax.axis_index("col")
     z, x = h // xs, h % xs
+
+    loads = [
+        pltpu.make_async_copy(part_ref.at[goal * xs + x], mine.at[goal], load_sem.at[goal])
+        for goal in range(zs)
+    ]
+    for load in loads:
+        load.start()
 
     barrier = pltpu.get_barrier_semaphore()
     for d in range(1, xs):
@@ -270,9 +326,11 @@
     for k in reversed(range(zs)):
         for d in range(1, xs):
             x_copy(k, d).start()
+    for load in loads:
+        load.wait()
     for k in reversed(range(zs)):
         goal = flip(z, k, zs)
-        value = part_ref[goal * xs + x].astype(jnp.float32)
+        value = mine[goal].astype(jnp.float32)
         for d in range(1, xs):
             other = (x + d) % xs
             pltpu.make_async_copy(
@@ -304,44 +362,52 @@
     entries = shells * top
     capacity = max(2, (entries + col_count - 1) // col_count)
     peers = row_count // CORES
-    message = (capacity, panels + TAIL, width)
+    message = (capacity * panels + TAIL, width)
     vmem = pl.BlockSpec(memory_space=pltpu.VMEM)
     smem = pl.BlockSpec(memory_space=pltpu.SMEM)
+    hbm = pl.BlockSpec(memory_space=pl.ANY)
     dma = pltpu.SemaphoreType.DMA
 
-    got = pl.pallas_call(
+    messages = row_count * col_count
+    got, ids = pl.pallas_call(
         functools.partial(exchange_kernel, row_count, col_count, capacity),
-        out_shape=jax.ShapeDtypeStruct((row_count, col_count) + message, jnp.bfloat16),
-        in_specs=[smem, smem, vmem, vmem],
-        out_specs=vmem,
+        out_shape=(
+            jax.ShapeDtypeStruct((row_count, col_count) + message, jnp.bfloat16),
+            jax.ShapeDtypeStruct((messages, width), jnp.int32),
+        ),
+        in_specs=[smem, smem, hbm, hbm],
+        out_specs=(hbm, vmem),
         scratch_shapes=[
+            pltpu.VMEM((entries, 2 * panels, depth), jnp.bfloat16),
+            pltpu.VMEM(shell_velocity.shape, jnp.bfloat16),
             pltpu.VMEM((col_count,) + message, jnp.bfloat16),
+            pltpu.VMEM((row_count, col_count, TAIL, width), jnp.bfloat16),
+            dma((2,)),
+            dma((1,)),
             dma((col_count,)),
             dma((peers, col_count)),
             dma((peers, col_count)),
             dma((row_count, col_count)),
         ],
         compiler_params=pltpu.CompilerParams(
-            collective_id=0, has_side_effects=True, vmem_limit_bytes=48 * 1024 * 1024
+            collective_id=0, has_side_effects=True, vmem_limit_bytes=56 * 1024 * 1024
         ),
         name="exchange",
     )(
-        coupling_dest.reshape(entries),
-        coupling_cluster.reshape(entries),
+        coupling_dest,
+        coupling_cluster,
         coupling.reshape(entries, 2 * panels, depth),
         shell_velocity,
     )
 
-    slots = row_count * col_count * capacity
-    got = got.reshape(slots, panels + TAIL, width)
-    ids = got[:, panels, 0].astype(jnp.int32)
+    got = got.reshape((messages,) + message)
     near_count, far_count, rank = near_blocks.shape[2], far_v.shape[2], far_v.shape[4]
     near = near_blocks.reshape(near_count, 2 * panels, panels)
     right = far_v.reshape(far_count, 2 * rank, panels)
     left = far_u.reshape(far_count, 2 * rank, panels)
     steps = 8
     partial_rows = pl.pallas_call(
-        functools.partial(field_kernel, steps),
+        functools.partial(field_kernel, steps, capacity),
         grid=(steps,),
         out_shape=jax.ShapeDtypeStruct((RC_DEV, panels, width), jnp.bfloat16),
         in_specs=[
@@ -355,9 +421,10 @@
         out_specs=pl.BlockSpec((RC_DEV, panels, width), lambda i: (0, 0, 0)),
         scratch_shapes=[
             pltpu.SMEM((CC_DEV,), jnp.int32),
-            pltpu.SMEM((slots,), jnp.int32),
+            pltpu.SMEM((messages * capacity,), jnp.int32),
             pltpu.VMEM((CC_DEV, panels, width), jnp.bfloat16),
             pltpu.VMEM((RC_DEV, 2 * panels, width), jnp.float32),
+            pltpu.VMEM((RC_DEV, panels, width), jnp.float32),
         ],
         compiler_params=pltpu.CompilerParams(vmem_limit_bytes=56 * 1024 * 1024),
         name="fields",
@@ -371,19 +438,21 @@
     return pl.pallas_call(
         functools.partial(reduce_kernel, zs, xs),
         out_shape=jax.ShapeDtypeStruct((out_rows, width), jnp.bfloat16),
-        in_specs=[vmem],
+        in_specs=[hbm],
         out_specs=vmem,
         scratch_shapes=[
+            pltpu.VMEM((zs, out_rows, width), jnp.bfloat16),
             pltpu.VMEM((zs, xs, out_rows, width), jnp.bfloat16),
             pltpu.VMEM((zs, out_rows, width), jnp.bfloat16),
             pltpu.VMEM((zs, out_rows, width), jnp.bfloat16),
+            dma((zs,)),
             dma((zs, xs)),
             dma((zs, xs)),
             dma((zs,)),
             dma((zs,)),
         ],
         compiler_params=pltpu.CompilerParams(
-            collective_id=1, has_side_effects=True, vmem_limit_bytes=32 * 1024 * 1024
+            collective_id=1, has_side_effects=True, vmem_limit_bytes=56 * 1024 * 1024
         ),
         name="reduce",
     )(partial_rows.reshape(col_count, out_rows, width))

time: 94.3 us -> 85.8 us (0.910)
  Pallas kernels: 85.3 us -> 81.1 us
  other arithmetic: 2.65 us -> 0 us
  local copies, waits for them, and re-layouts: 6.1 us -> 4.25 us
    pallas_call x1, Pallas kernels: 23.7 us -> 17.3 us  [per_device(): pl.pallas_call(functools.partial(field_kernel, steps, capacity), grid=(st...]
    convert_element_type x1 -> x0, other arithmetic: 2.65 us -> none  [per_device(): ids = got[:, panels, 0].astype(jnp.int32)]
    pallas_call x1, Pallas kernels: 40.4 us -> 42.4 us  [per_device(): pl.pallas_call(functools.partial(exchange_kernel, row_count, col_count, c...]
    unnamed x9 -> x3, local copies, waits for them, and re-layouts: 5.93 us -> 4.25 us
where the time goes in v2:
time: 85.8 us; the launch traced here: 85.4 us
  Pallas kernels  81.1 us (95%)
  local copies, waits for them, and re-layouts  4.25 us (5%)
    pallas_call x1, Pallas kernels, per_device(): pl.pallas_call(functools.partial(exchange_kernel, row_count, col_count, c...  42.4 us
    pallas_call x1, Pallas kernels, per_device(): pl.pallas_call(functools.partial(reduce_kernel, zs, xs), out_shape=jax.Sh...  21.4 us
    pallas_call x1, Pallas kernels, per_device(): pl.pallas_call(functools.partial(field_kernel, steps, capacity), grid=(st...  17.3 us
    unnamed x3, local copies, waits for them, and re-layouts  4.25 us

profile of v2, /device:TPU:0, one launch (start us, length us, event | category | flops | bytes accessed | tf_op | source)
XLA Modules:
  0.0 85.4 jit_solution(7759777722197232707)
XLA Ops:
  0.0 1.3 %copy.9.dest_ref = s32[8,2]{1,0:T(8,128)} copy(s32[8,2]{0,1:T(2,128)} %param.10) | data formatting | bytes 128 | tf_op args[2]
  1.3 1.3 %copy.10.cluster_ref = s32[8,2]{1,0:T(8,128)} copy(s32[8,2]{0,1:T(2,128)} %param.11) | data formatting | bytes 128 | tf_op args[3]
  2.7 42.4 %exchange.1 = (bf16[4,8,528,128]{3,2,1,0:T(8,128)(2,1)}, s32[32,128]{1,0:T(8,128)}) custom-call(s32[8,2]{1,0:T(8,128)} %copy.9.dest_ref, s32[8,2]{1,0:T(8,128)} %copy.10.cluster_ref, bf16[16,512,128]{2,1,0:T(8,128)(2,1)} %bitcast.12, bf16[8,128,128]{2,1,0:T(8,128)(2,1)} %velocity_hbm.1), custom_call_target="tpu_custom_call" | custom-call | tf_op jit(solution)/shard_map/exchange/pallas_call | solution.py:372
  45.1 17.3 %fields.1 = bf16[16,256,128]{2,1,0:T(8,128)(2,1)} custom-call(s32[32,128]{1,0:T(8,128)} %get-tuple-element.7.ids_ref, s32[96]{0:T(128)} %bitcast.13, bf16[32,528,128]{2,1,0:T(8,128)(2,1)} %bitcast.8, bf16[32,512,256]{2,1,0:T(8,128)(2,1)} %bitcast.7, bf16[64,64,256]{2,1,0:T(8,128)(2,1)} %bitcast.10, bf16[64,64,256]{2,1,0:T(8,128)(2,1)} %bitcast.11), custom_call_target="tpu_custom_call" | custom-call | tf_op jit(solution)/shard_map/fields/pallas_call | solution.py:409
  62.4 21.4 %reduce.1 = bf16[512,128]{1,0:T(8,128)(2,1)} custom-call(bf16[8,512,128]{2,1,0:T(8,128)(2,1)} %bitcast.9), custom_call_target="tpu_custom_call" | custom-call | tf_op jit(solution)/shard_map/reduce/pallas_call | solution.py:438
  83.8 1.6 %copy.12 = bf16[512,128]{1,0:T(8,128)(2,1)} copy(bf16[512,128]{1,0:T(8,128)(2,1)} %reduce.1) | data formatting | bytes 262144

commit v3 on v2

--- a/solution.py
+++ b/solution.py
@@ -11,6 +11,7 @@
 CC_DEV = 64
 NEAR_DEV = 32
 CORES = 2
+PIECES = 2
 TAIL = 16
 MESH = pl.DeviceIdType.MESH
 
@@ -62,124 +63,124 @@
     for load in loads:
         load.wait()
 
-    def fill(j):
+    def rows_of(k):
+        return pl.ds(0, TAIL + panels) if k == 0 else pl.ds(TAIL + k * panels, panels)
+
+    def fill(j, send):
         target = flip(h, j, cols)
         picked = [jnp.int32(-1)] * capacity
         count = jnp.int32(0)
         for e in range(entries):
-            hit = dest_ref[e // top, e % top] == target
+            hit = dest_ref[e % top, e // top] == target
             for k in range(capacity):
                 picked[k] = jnp.where(hit & (count == k), e, picked[k])
             count = count + jnp.where(hit, 1, 0)
         lane = lax.broadcasted_iota(jnp.int32, (TAIL, width), 1)
         tail = jnp.zeros((TAIL, width), jnp.float32)
         for k in range(capacity):
-            valid = picked[k] >= 0
+            e = jnp.maximum(picked[k], 0)
+            number = jnp.where(picked[k] >= 0, cluster_ref[e % top, e // top], 0)
+            tail = jnp.where(lane == k, number.astype(jnp.float32), tail)
+        outgoing[j, pl.ds(0, TAIL), :] = tail.astype(jnp.bfloat16)
+        for k in range(capacity):
             e = jnp.maximum(picked[k], 0)
             product = jnp.dot(
                 coupling_ref[e], velocity_ref[e // top], preferred_element_type=jnp.float32
             )
             value = product[:panels] + rotate(product[panels:])
-            scale = jnp.where(valid, 1.0, 0.0)
-            outgoing[j, pl.ds(k * panels, panels), :] = (value * scale).astype(jnp.bfloat16)
-            number = jnp.where(valid, cluster_ref[e // top, e % top], 0).astype(jnp.float32)
-            tail = jnp.where(lane == k, number, tail)
-        outgoing[j, pl.ds(capacity * panels, TAIL), :] = tail.astype(jnp.bfloat16)
-
-    def col_copy(j):
+            scale = jnp.where(picked[k] >= 0, 1.0, 0.0)
+            outgoing[j, pl.ds(TAIL + k * panels, panels), :] = (value * scale).astype(jnp.bfloat16)
+            send(k)
+
+    def col_copy(j, k):
         target = flip(h, j, cols)
         return pltpu.make_async_remote_copy(
-            src_ref=outgoing.at[j],
-            dst_ref=got_ref.at[g, h],
-            send_sem=send_col.at[j],
-            recv_sem=recv.at[g, h],
+            src_ref=outgoing.at[j, rows_of(k), :],
+            dst_ref=got_ref.at[g, h, rows_of(k), :],
+            send_sem=send_col.at[j, k],
+            recv_sem=recv.at[g, h, k],
             device_id=(g, target),
             device_id_type=MESH,
         )
 
-    def relay_copy(origin, source, block, send_sem, row):
+    def relay_copy(origin, source, k, own, send_sem, row):
+        block = outgoing.at[0, rows_of(k), :] if own else got_ref.at[origin, source, rows_of(k), :]
         return pltpu.make_async_remote_copy(
             src_ref=block,
-            dst_ref=got_ref.at[origin, source],
+            dst_ref=got_ref.at[origin, source, rows_of(k), :],
             send_sem=send_sem,
-            recv_sem=recv.at[origin, source],
+            recv_sem=recv.at[origin, source, k],
             device_id=(row, h),
             device_id_type=MESH,
         )
 
-    def y_copy(step, j, block=None):
+    def y_copy(step, j, k, own=False):
         source = flip(h, j, cols)
-        return relay_copy(
-            g, source, got_ref.at[g, source] if block is None else block,
-            send_y.at[step, j], (y + step) % peers * CORES + core,
-        )
-
-    def core_copy(step, j, block=None):
+        row = (y + step) % peers * CORES + core
+        return relay_copy(g, source, k, own, send_y.at[step, j, k], row)
+
+    def core_copy(step, j, k, own=False):
         source = flip(h, j, cols)
         origin = (y + step) % peers * CORES + core
-        return relay_copy(
-            origin, source, got_ref.at[origin, source] if block is None else block,
-            send_core.at[step, j], mate,
-        )
-
-    def arrived(origin, j):
-        source = flip(h, j, cols)
-        pltpu.make_async_copy(
-            got_ref.at[origin, source], got_ref.at[origin, source], recv.at[origin, source]
-        ).wait()
-
-    fill(0)
-    own = pltpu.make_async_copy(outgoing.at[0], got_ref.at[g, h], send_col.at[0])
+        return relay_copy(origin, source, k, own, send_core.at[step, j, k], mate)
+
+    def arrived(origin, j, k):
+        block = got_ref.at[origin, flip(h, j, cols), rows_of(k), :]
+        pltpu.make_async_copy(block, block, recv.at[origin, flip(h, j, cols), k]).wait()
+
+    def hand_out(k):
+        for step in range(1, peers):
+            y_copy(step, 0, k, True).start()
+        core_copy(0, 0, k, True).start()
+
+    fill(0, lambda k: None)
+    own = pltpu.make_async_copy(outgoing.at[0], got_ref.at[g, h], tail_sem.at[0])
     own.start()
     pl.semaphore_wait(barrier, cols - 1 + peers - 1 + 1)
-    for step in range(1, peers):
-        y_copy(step, 0, outgoing.at[0]).start()
-    core_copy(0, 0, outgoing.at[0]).start()
-
-    half = cols // 2
+    for k in range(capacity):
+        hand_out(k)
 
     @pl.loop(1, cols)
-    def _(i):
-        j = (i % 2) * half + i // 2
-        fill(j)
-        col_copy(j).start()
+    def _(j):
+        fill(j, lambda k: col_copy(j, k).start())
 
     lag = cols // 2
 
-    def pass_on(i):
-        j = (i % 2) * half + i // 2
-        arrived(g, j)
-        for step in range(1, peers):
-            y_copy(step, j).start()
-        core_copy(0, j).start()
-
-    def relay(i):
-        j = (i % 2) * half + i // 2
-        for step in range(1, peers):
-            arrived((y + step) % peers * CORES + core, j)
-            core_copy(step, j).start()
+    def pass_on(j):
+        for k in range(capacity):
+            arrived(g, j, k)
+            for step in range(1, peers):
+                y_copy(step, j, k).start()
+            core_copy(0, j, k).start()
+
+    def relay(j):
+        for k in range(capacity):
+            for step in range(1, peers):
+                arrived((y + step) % peers * CORES + core, j, k)
+                core_copy(step, j, k).start()
 
     @pl.loop(1, lag)
-    def _(i):
-        pass_on(i)
+    def _(j):
+        pass_on(j)
 
     @pl.loop(lag, cols)
-    def _(i):
-        pass_on(i)
-        relay(i - lag)
+    def _(j):
+        pass_on(j)
+        relay(j - lag)
 
     @pl.loop(cols - lag, cols)
-    def _(i):
-        relay(i)
+    def _(j):
+        relay(j)
 
     @pl.loop(0, cols)
     def _(j):
         for step in range(peers):
-            arrived((y + step) % peers * CORES + (CORES - 1 - core), j)
+            for k in range(capacity):
+                arrived((y + step) % peers * CORES + (CORES - 1 - core), j, k)
 
     own.wait()
     gather = pltpu.make_async_copy(
-        got_ref.at[:, :, pl.ds(capacity * panels, TAIL), :], tails, tail_sem.at[0]
+        got_ref.at[:, :, pl.ds(0, TAIL), :], tails, tail_sem.at[1]
     )
     gather.start()
     gather.wait()
@@ -189,20 +190,22 @@
 
     @pl.loop(1, cols)
     def _(j):
-        col_copy(j).wait_send()
-
-    for step in range(1, peers):
-        y_copy(step, 0, outgoing.at[0]).wait_send()
-    core_copy(0, 0, outgoing.at[0]).wait_send()
-    for step in range(1, peers):
-        core_copy(step, 0).wait_send()
+        for k in range(capacity):
+            col_copy(j, k).wait_send()
+
+    for k in range(capacity):
+        for step in range(1, peers):
+            y_copy(step, 0, k, True).wait_send()
+            core_copy(step, 0, k).wait_send()
+        core_copy(0, 0, k, True).wait_send()
 
     @pl.loop(1, cols)
     def _(j):
-        for step in range(1, peers):
-            y_copy(step, j).wait_send()
-        for step in range(peers):
-            core_copy(step, j).wait_send()
+        for k in range(capacity):
+            for step in range(1, peers):
+                y_copy(step, j, k).wait_send()
+            for step in range(peers):
+                core_copy(step, j, k).wait_send()
 
 
 def field_kernel(
@@ -235,7 +238,7 @@
 
             def add(state):
                 n, value = state
-                start = pl.multiple_of(n % capacity * panels, panels)
+                start = pl.multiple_of(TAIL + n % capacity * panels, TAIL)
                 block = got_ref[n // capacity, pl.ds(start, panels), :]
                 return link[n], value + block.astype(jnp.float32)
 
@@ -301,55 +304,64 @@
         )
     pl.semaphore_wait(barrier, xs - 1 + zs - 1)
 
-    def x_copy(k, d):
+    rows = out_ref.shape[0] // PIECES
+    parts = [pl.ds(p * rows, rows) for p in range(PIECES)]
+
+    def x_copy(k, d, p):
         goal, other = flip(z, k, zs), (x + d) % xs
         return pltpu.make_async_remote_copy(
-            src_ref=part_ref.at[goal * xs + other],
-            dst_ref=first.at[goal, x],
-            send_sem=send1.at[goal, other],
-            recv_sem=recv1.at[goal, x],
+            src_ref=part_ref.at[goal * xs + other, parts[p], :],
+            dst_ref=first.at[goal, x, parts[p], :],
+            send_sem=send1.at[goal, other, p],
+            recv_sem=recv1.at[goal, x, p],
             device_id=(g, z * xs + other),
             device_id_type=MESH,
         )
 
-    def z_copy(k):
+    def z_copy(k, p):
         goal = flip(z, k, zs)
         return pltpu.make_async_remote_copy(
-            src_ref=middle.at[goal],
-            dst_ref=second.at[z],
-            send_sem=send2.at[goal],
-            recv_sem=recv2.at[z],
+            src_ref=middle.at[goal, parts[p], :],
+            dst_ref=second.at[z, parts[p], :],
+            send_sem=send2.at[goal, p],
+            recv_sem=recv2.at[z, p],
             device_id=(g, goal * xs + x),
             device_id_type=MESH,
         )
 
-    for k in reversed(range(zs)):
+    order = [(k, p) for k in reversed(range(zs)) for p in range(PIECES)]
+    for k, p in order:
         for d in range(1, xs):
-            x_copy(k, d).start()
+            x_copy(k, d, p).start()
     for load in loads:
         load.wait()
-    for k in reversed(range(zs)):
+    totals = [None] * PIECES
+    for k, p in order:
         goal = flip(z, k, zs)
-        value = mine[goal].astype(jnp.float32)
+        value = mine[goal, parts[p], :].astype(jnp.float32)
         for d in range(1, xs):
             other = (x + d) % xs
-            pltpu.make_async_copy(
-                first.at[goal, other], first.at[goal, other], recv1.at[goal, other]
-            ).wait()
-            value = value + first[goal, other].astype(jnp.float32)
+            block = first.at[goal, other, parts[p], :]
+            pltpu.make_async_copy(block, block, recv1.at[goal, other, p]).wait()
+            value = value + first[goal, other, parts[p], :].astype(jnp.float32)
         if k:
-            middle[goal] = value.astype(jnp.bfloat16)
-            z_copy(k).start()
-    for k in range(1, zs):
-        source = flip(z, k, zs)
-        pltpu.make_async_copy(second.at[source], second.at[source], recv2.at[source]).wait()
-        value = value + second[source].astype(jnp.float32)
-    out_ref[...] = value.astype(jnp.bfloat16)
-    for k in range(zs):
+            middle[goal, parts[p], :] = value.astype(jnp.bfloat16)
+            z_copy(k, p).start()
+        else:
+            totals[p] = value
+    for p in range(PIECES):
+        value = totals[p]
+        for k in range(1, zs):
+            source = flip(z, k, zs)
+            block = second.at[source, parts[p], :]
+            pltpu.make_async_copy(block, block, recv2.at[source, p]).wait()
+            value = value + second[source, parts[p], :].astype(jnp.float32)
+        out_ref[parts[p], :] = value.astype(jnp.bfloat16)
+    for k, p in order:
         for d in range(1, xs):
-            x_copy(k, d).wait_send()
+            x_copy(k, d, p).wait_send()
         if k:
-            z_copy(k).wait_send()
+            z_copy(k, p).wait_send()
 
 
 def per_device(
@@ -383,19 +395,19 @@
             pltpu.VMEM((col_count,) + message, jnp.bfloat16),
             pltpu.VMEM((row_count, col_count, TAIL, width), jnp.bfloat16),
             dma((2,)),
-            dma((1,)),
-            dma((col_count,)),
-            dma((peers, col_count)),
-            dma((peers, col_count)),
-            dma((row_count, col_count)),
+            dma((2,)),
+            dma((col_count, capacity)),
+            dma((peers, col_count, capacity)),
+            dma((peers, col_count, capacity)),
+            dma((row_count, col_count, capacity)),
         ],
         compiler_params=pltpu.CompilerParams(
             collective_id=0, has_side_effects=True, vmem_limit_bytes=56 * 1024 * 1024
         ),
         name="exchange",
     )(
-        coupling_dest,
-        coupling_cluster,
+        coupling_dest.T,
+        coupling_cluster.T,
         coupling.reshape(entries, 2 * panels, depth),
         shell_velocity,
     )
@@ -438,7 +450,7 @@
     return pl.pallas_call(
         functools.partial(reduce_kernel, zs, xs),
         out_shape=jax.ShapeDtypeStruct((out_rows, width), jnp.bfloat16),
-        in_specs=[hbm],
+        in_specs=[pl.BlockSpec(memory_space=pltpu.HBM)],
         out_specs=vmem,
         scratch_shapes=[
             pltpu.VMEM((zs, out_rows, width), jnp.bfloat16),
@@ -446,10 +458,10 @@
             pltpu.VMEM((zs, out_rows, width), jnp.bfloat16),
             pltpu.VMEM((zs, out_rows, width), jnp.bfloat16),
             dma((zs,)),
-            dma((zs, xs)),
-            dma((zs, xs)),
-            dma((zs,)),
-            dma((zs,)),
+            dma((zs, xs, PIECES)),
+            dma((zs, xs, PIECES)),
+            dma((zs, PIECES)),
+            dma((zs, PIECES)),
         ],
         compiler_params=pltpu.CompilerParams(
             collective_id=1, has_side_effects=True, vmem_limit_bytes=56 * 1024 * 1024

time: 85.8 us -> 79.8 us (0.930)
  Pallas kernels: 81.1 us -> 77.9 us
  local copies, waits for them, and re-layouts: 4.25 us -> 1.57 us
    pallas_call x1, Pallas kernels: 42.4 us -> 39.1 us  [per_device(): pl.pallas_call(functools.partial(exchange_kernel, row_count, col_count, c...]
    unnamed x3 -> x1, local copies, waits for them, and re-layouts: 4.25 us -> 1.57 us
where the time goes in v3:
time: 79.8 us; the launch traced here: 79.5 us
  Pallas kernels  77.9 us (98%)
  local copies, waits for them, and re-layouts  1.57 us (2%)
    pallas_call x1, Pallas kernels, per_device(): pl.pallas_call(functools.partial(exchange_kernel, row_count, col_count, c...  39.1 us
    pallas_call x1, Pallas kernels, per_device(): pl.pallas_call(functools.partial(reduce_kernel, zs, xs), out_shape=jax.Sh...  21.6 us
    pallas_call x1, Pallas kernels, per_device(): pl.pallas_call(functools.partial(field_kernel, steps, capacity), grid=(st...  17.3 us

profile of v3, /device:TPU:0, one launch (start us, length us, event | category | flops | bytes accessed | tf_op | source)
XLA Modules:
  0.0 79.5 jit_solution(17211469385803159692)
XLA Ops:
  0.0 39.1 %exchange.1 = (bf16[4,8,528,128]{3,2,1,0:T(8,128)(2,1)}, s32[32,128]{1,0:T(8,128)}) custom-call(s32[2,8]{1,0:T(2,128)} %bitcast.15, s32[2,8]{1,0:T(2,128)} %bitcast.16, bf16[16,512,128]{2,1,0:T(8,128)(2,1)} %bitcast.14, bf16[8,128,128]{2,1,0:T(8,128)(2,1)} %velocity_hbm.1), custom_call_target="tpu_custom_call" | custom-call | tf_op jit(solution)/shard_map/exchange/pallas_call | solution.py:384
  39.1 17.3 %fields.1 = bf16[16,256,128]{2,1,0:T(8,128)(2,1)} custom-call(s32[32,128]{1,0:T(8,128)} %get-tuple-element.7.ids_ref, s32[96]{0:T(128)} %bitcast.17, bf16[32,528,128]{2,1,0:T(8,128)(2,1)} %bitcast.10, bf16[32,512,256]{2,1,0:T(8,128)(2,1)} %bitcast.9, bf16[64,64,256]{2,1,0:T(8,128)(2,1)} %bitcast.12, bf16[64,64,256]{2,1,0:T(8,128)(2,1)} %bitcast.13), custom_call_target="tpu_custom_call" | custom-call | tf_op jit(solution)/shard_map/fields/pallas_call | solution.py:421
  56.3 21.6 %reduce.1 = bf16[512,128]{1,0:T(8,128)(2,1)} custom-call(bf16[8,512,128]{2,1,0:T(8,128)(2,1)} %bitcast.11), custom_call_target="tpu_custom_call" | custom-call | tf_op jit(solution)/shard_map/reduce/pallas_call | solution.py:450
  77.9 1.6 %copy.10 = bf16[512,128]{1,0:T(8,128)(2,1)} copy(bf16[512,128]{1,0:T(8,128)(2,1)} %reduce.1) | data formatting | bytes 262144

commit v4 on v3

--- a/solution.py
+++ b/solution.py
@@ -11,7 +11,7 @@
 CC_DEV = 64
 NEAR_DEV = 32
 CORES = 2
-PIECES = 2
+PIECES = 4
 TAIL = 16
 MESH = pl.DeviceIdType.MESH
 
@@ -233,19 +233,36 @@
 
         @pl.loop(0, CC_DEV)
         def _(c):
-            def more(state):
-                return state[0] >= 0
-
-            def add(state):
-                n, value = state
+            def block(n):
                 start = pl.multiple_of(TAIL + n % capacity * panels, TAIL)
-                block = got_ref[n // capacity, pl.ds(start, panels), :]
-                return link[n], value + block.astype(jnp.float32)
-
-            _, value = lax.while_loop(
-                more, add, (head[c], jnp.zeros((panels, width), jnp.float32))
-            )
-            sources[c] = value.astype(jnp.bfloat16)
+                return got_ref[n // capacity, pl.ds(start, panels), :]
+
+            one = head[c]
+            two = jnp.where(one >= 0, link[jnp.maximum(one, 0)], -1)
+            three = jnp.where(two >= 0, link[jnp.maximum(two, 0)], -1)
+
+            @pl.when(one < 0)
+            def _():
+                sources[c] = jnp.zeros((panels, width), jnp.bfloat16)
+
+            @pl.when((one >= 0) & (two < 0))
+            def _():
+                sources[c] = block(one)
+
+            @pl.when((two >= 0) & (three < 0))
+            def _():
+                value = block(one).astype(jnp.float32) + block(two).astype(jnp.float32)
+                sources[c] = value.astype(jnp.bfloat16)
+
+            @pl.when(three >= 0)
+            def _():
+                def add(state):
+                    n, value = state
+                    return link[n], value + block(n).astype(jnp.float32)
+
+                value = block(one).astype(jnp.float32) + block(two).astype(jnp.float32)
+                _, value = lax.while_loop(lambda state: state[0] >= 0, add, (three, value))
+                sources[c] = value.astype(jnp.bfloat16)
 
         near_total[...] = jnp.zeros_like(near_total)
         far_total[...] = jnp.zeros_like(far_total)

time: 79.8 us -> 80.3 us (level)
  no operation moved by 1% of the time
where the time goes in v4:
time: 80.3 us; the launch traced here: 79.9 us
  Pallas kernels  78.4 us (98%)
  local copies, waits for them, and re-layouts  1.57 us (2%)
    pallas_call x1, Pallas kernels, per_device(): pl.pallas_call(functools.partial(exchange_kernel, row_count, col_count, c...  39.1 us
    pallas_call x1, Pallas kernels, per_device(): pl.pallas_call(functools.partial(reduce_kernel, zs, xs), out_shape=jax.Sh...  21.6 us
    pallas_call x1, Pallas kernels, per_device(): pl.pallas_call(functools.partial(field_kernel, steps, capacity), grid=(st...  17.7 us

profile of v4, /device:TPU:0, one launch (start us, length us, event | category | flops | bytes accessed | tf_op | source)
XLA Modules:
  0.0 79.9 jit_solution(6785417126501359472)
XLA Ops:
  0.0 39.1 %exchange.1 = (bf16[4,8,528,128]{3,2,1,0:T(8,128)(2,1)}, s32[32,128]{1,0:T(8,128)}) custom-call(s32[2,8]{1,0:T(2,128)} %bitcast.15, s32[2,8]{1,0:T(2,128)} %bitcast.16, bf16[16,512,128]{2,1,0:T(8,128)(2,1)} %bitcast.14, bf16[8,128,128]{2,1,0:T(8,128)(2,1)} %velocity_hbm.1), custom_call_target="tpu_custom_call" | custom-call | tf_op jit(solution)/shard_map/exchange/pallas_call | solution.py:401
  39.1 17.7 %fields.1 = bf16[16,256,128]{2,1,0:T(8,128)(2,1)} custom-call(s32[32,128]{1,0:T(8,128)} %get-tuple-element.7.ids_ref, s32[96]{0:T(128)} %bitcast.17, bf16[32,528,128]{2,1,0:T(8,128)(2,1)} %bitcast.10, bf16[32,512,256]{2,1,0:T(8,128)(2,1)} %bitcast.9, bf16[64,64,256]{2,1,0:T(8,128)(2,1)} %bitcast.12, bf16[64,64,256]{2,1,0:T(8,128)(2,1)} %bitcast.13), custom_call_target="tpu_custom_call" | custom-call | tf_op jit(solution)/shard_map/fields/pallas_call | solution.py:438
  56.8 21.6 %reduce.1 = bf16[512,128]{1,0:T(8,128)(2,1)} custom-call(bf16[8,512,128]{2,1,0:T(8,128)(2,1)} %bitcast.11), custom_call_target="tpu_custom_call" | custom-call | tf_op jit(solution)/shard_map/reduce/pallas_call | solution.py:467
  78.4 1.6 %copy.10 = bf16[512,128]{1,0:T(8,128)(2,1)} copy(bf16[512,128]{1,0:T(8,128)(2,1)} %reduce.1) | data formatting | bytes 262144
